TPU v7x, 512 devices: a whole 4x8x8 slice. The times are simulated.
512 devices in a mesh: expert: 64 (over z, y), tensor: 8 (over x, core).
Axes of the slice: x: 4, y: 8, z: 8, core: 2. Of those that a mesh axis runs over, the one named last changes fastest.
Arguments:
- tokens: bfloat16 [3072, 4096], P('expert', 'tensor'), may hold values from -6 to 6
- cotangent: bfloat16 [3072, 4096], P('expert', 'tensor'), may hold values from -6 to 6
- expert_ids: int32 [3072, 8], P('expert'), may hold values from 0 to 63, all different within a row; in each aligned block of 48 rows (0 to 47, 48 to 95, ...) at most 8 rows name the same one
- gate_values: float32 [3072, 8], P('expert'), may hold values from 0.05 to 1
- w_gate: bfloat16 [64, 768, 4096], P('expert', 'tensor'), may hold values from -0.09375 to 0.09375
- w_up: bfloat16 [64, 768, 4096], P('expert', 'tensor'), may hold values from -0.09375 to 0.09375
- w_down: bfloat16 [64, 768, 4096], P('expert', 'tensor'), may hold values from -0.21875 to 0.21875
Outputs:
- grad_tokens: bfloat16 [3072, 4096], P('expert', 'tensor')
- grad_gate: bfloat16 [64, 768, 4096], P('expert', 'tensor')
- grad_up: bfloat16 [64, 768, 4096], P('expert', 'tensor')
- grad_down: bfloat16 [64, 768, 4096], P('expert', 'tensor')
Inputs may be any that keep to these rules, and one draw needn't show every extreme that they name: `expert_ids`: each row names 8 different experts. Among the 48 tokens of one index of the expert axis no expert is named more than 8 times, and in every draw some expert is named exactly 8 times there.
All inputs are finite; a program needn't handle non-finite values.
Results may differ from a plain program's by a relative error of at most 0.019.
Values may be sent and summed in bfloat16 or wider, within the bound.
No kernel may reach another device: no remote copies, remote signals or barrier semaphores. Data moves between devices by JAX's collectives and lax.ppermute only.
A program may use at most 64 MiB of HBM per device.

v0:
```python
import jax
import jax.numpy as jnp
from jax import lax
from jax.sharding import PartitionSpec as P

TOP = 8


def expert_backward(rows_x, rows_d, w_gate, w_up, w_down):
    gate_pre = jnp.einsum("secd,ehd->sech", rows_x, w_gate, preferred_element_type=jnp.float32)
    up_pre = jnp.einsum("secd,ehd->sech", rows_x, w_up, preferred_element_type=jnp.float32)
    sigmoid = jax.nn.sigmoid(gate_pre)
    active = gate_pre * sigmoid
    hidden = (active * up_pre).astype(jnp.bfloat16)
    hidden_grad = jnp.einsum("secd,ehd->sech", rows_d, w_down, preferred_element_type=jnp.float32)
    up_grad = (hidden_grad * active).astype(jnp.bfloat16)
    gate_grad = (hidden_grad * up_pre * sigmoid * (1.0 + gate_pre * (1.0 - sigmoid))).astype(
        jnp.bfloat16
    )
    grad_gate = jnp.einsum(
        "sech,secd->ehd", gate_grad, rows_x, preferred_element_type=jnp.float32
    ).astype(jnp.bfloat16)
    grad_up = jnp.einsum(
        "sech,secd->ehd", up_grad, rows_x, preferred_element_type=jnp.float32
    ).astype(jnp.bfloat16)
    grad_down = jnp.einsum(
        "sech,secd->ehd", hidden, rows_d, preferred_element_type=jnp.float32
    ).astype(jnp.bfloat16)
    partial_value = jnp.einsum(
        "sech,ehd->secd", gate_grad, w_gate, preferred_element_type=jnp.float32
    )
    partial_value = partial_value + jnp.einsum(
        "sech,ehd->secd", up_grad, w_up, preferred_element_type=jnp.float32
    )
    return (partial_value, grad_gate, grad_up, grad_down)


def on_device(tokens, cotangent, expert_ids, gate_values, w_gate, w_up, w_down):
    tok_count = expert_ids.shape[0]
    local_count = w_gate.shape[0]
    groups = lax.axis_size("expert")
    experts = local_count * groups
    capacity = 4 * tok_count * TOP // (3 * experts)
    feat_width = tokens.shape[1]
    flat_ids = expert_ids.reshape(-1)
    onehot = (flat_ids[:, None] == jnp.arange(experts, dtype=jnp.int32)[None, :]).astype(jnp.int32)
    before = jnp.cumsum(onehot, axis=0) - onehot
    slot_pos = jnp.sum(before * onehot, axis=1)
    target = flat_ids * capacity + slot_pos
    matches = (target[None, :] == jnp.arange(experts * capacity, dtype=jnp.int32)[:, None]).reshape(
        experts * capacity, tok_count, TOP
    )
    by_token = jnp.any(matches, axis=2)
    occupied = jnp.any(by_token, axis=1)
    token_iota = jnp.arange(tok_count, dtype=jnp.int32)
    owner = jnp.sum(jnp.where(by_token, token_iota[None, :], 0), axis=1)
    slot_weight = jnp.sum(jnp.sum(jnp.where(matches, gate_values[None, :, :], 0.0), axis=2), axis=1)
    full_x, full_d = (
        lax.all_gather(tokens, "tensor", axis=1, tiled=True),
        lax.all_gather(cotangent, "tensor", axis=1, tiled=True),
    )
    sent_x = jnp.where(occupied[:, None], full_x[owner], jnp.zeros((), jnp.bfloat16))
    sent_d = (slot_weight[:, None] * full_d[owner].astype(jnp.float32)).astype(jnp.bfloat16)
    buffer_shape = (groups, local_count, capacity, full_x.shape[1])
    sent_x, sent_d = (sent_x.reshape(buffer_shape), sent_d.reshape(buffer_shape))
    rows_x, rows_d = (
        lax.all_to_all(sent_x, "expert", split_axis=0, concat_axis=0, tiled=True),
        lax.all_to_all(sent_d, "expert", split_axis=0, concat_axis=0, tiled=True),
    )
    partial_value, grad_gate, grad_up, grad_down = expert_backward(
        rows_x, rows_d, w_gate, w_up, w_down
    )
    summed = lax.psum(partial_value.astype(jnp.bfloat16), "tensor").astype(jnp.float32)
    returned = lax.dynamic_slice_in_dim(
        summed, lax.axis_index("tensor") * feat_width, feat_width, 3
    ).astype(jnp.bfloat16)
    arrived = lax.all_to_all(returned, "expert", split_axis=0, concat_axis=0, tiled=True).reshape(
        experts * capacity, feat_width
    )
    masked = jnp.where(occupied[:, None], arrived.astype(jnp.float32), jnp.zeros((), jnp.float32))
    grad_tokens = jax.ops.segment_sum(masked, owner, num_segments=tok_count).astype(jnp.bfloat16)
    return (grad_tokens, grad_gate, grad_up, grad_down)


def solution(mesh):
    return jax.shard_map(
        on_device,
        mesh=mesh,
        in_specs=(
            P("expert", "tensor"),
            P("expert", "tensor"),
            P("expert", None),
            P("expert", None),
            P("expert", "tensor", None),
            P("expert", "tensor", None),
            P("expert", "tensor", None),
        ),
        out_specs=(
            P("expert", "tensor"),
            P("expert", "tensor", None),
            P("expert", "tensor", None),
            P("expert", "tensor", None),
        ),
        check_vma=False,
    )
```

profile of v0, /device:TPU:15, one launch (start us, length us, event | category | flops | bytes accessed | tf_op | source)
XLA Modules:
  0.0 448.9 jit_solution(7881900945583448381)
XLA Ops:
  8.2 0.9 reduce-window.6
  11.0 13.7 %all_gather.7 = bf16[48,4096]{1,0:T(8,128)(2,1)S(1)} all-gather(bf16[48,512]{1,0:T(8,128)(2,1)} %param.7), channel_id=1, replica_groups=mesh['expert'=64,'tensor'=8] {'tensor'}, dimensions={1}, use_global_device_ids=true | all-gather | bytes 442368 | tf_op jit(solution)/shard_map/all_gather | solution.py:59
  24.6 4.3 gather_fusion.1
  29.0 4.5 %bitcast_select_fusion = bf16[64,1,8,4096]{3,2,1,0:T(8,128)(2,1)} fusion(bf16[512,4096]{1,0:T(8,128)(2,1)} %gather_fusion.1, pred[64,8]{1,0:T(8,128)(4,1)S(1)} %broadcast_in_dim.73), kind=kLoop, calls=%fused_computation.16 | loop fusion | flops 2097152 | bytes 8389120 | tf_op jit(solution)/shard_map/jit(_where)/select_n | solution.py:62
  33.5 16.3 %all-to-all-start.1 = ((bf16[64,1,8,4096]{3,2,1,0:T(8,128)(2,1)}), bf16[64,1,8,4096]{3,2,1,0:T(8,128)(2,1)}, u32[]{:S(2)}, u32[]{:S(2)}) async-start(bf16[64,1,8,4096]{3,2,1,0:T(8,128)(2,1)} %bitcast_select_fusion), calls=%async_computation.1 | async-start | bytes 8388608 | tf_op jit(solution)/shard_map/all_to_all | solution.py:67
  50.2 13.5 %all_gather.6 = bf16[48,4096]{1,0:T(8,128)(2,1)S(1)} all-gather(bf16[48,512]{1,0:T(8,128)(2,1)S(1)} %copy-done.2), channel_id=1, replica_groups=mesh['expert'=64,'tensor'=8] {'tensor'}, dimensions={1}, use_global_device_ids=true | all-gather | bytes 442368 | tf_op jit(solution)/shard_map/all_gather | solution.py:60
  63.8 4.4 gather_fusion
  68.1 5.6 %fusion = bf16[64,1,8,4096]{3,2,1,0:T(8,128)(2,1)} fusion(bf16[512,4096]{1,0:T(8,128)(2,1)} %gather_fusion, f32[64,8]{1,0:T(8,128)S(1)} %mul.57), kind=kLoop, calls=%fused_computation.4 | loop fusion | flops 6291456 | bytes 8390656 | tf_op jit(solution)/shard_map/convert_element_type | solution.py:63
  73.8 84.2 %all-to-all-done.1 = bf16[64,1,8,4096]{3,2,1,0:T(8,128)(2,1)} async-done(((bf16[64,1,8,4096]{3,2,1,0:T(8,128)(2,1)}), bf16[64,1,8,4096]{3,2,1,0:T(8,128)(2,1)}, u32[]{:S(2)}, u32[]{:S(2)}) %all-to-all-start.1) | async-done | bytes 4194336 | tf_op jit(solution)/shard_map/all_to_all | solution.py:67
  158.0 33.7 %all-to-all-start = ((bf16[64,1,8,4096]{3,2,1,0:T(8,128)(2,1)}), bf16[64,1,8,4096]{3,2,1,0:T(8,128)(2,1)}, u32[]{:S(2)}, u32[]{:S(2)}) async-start(bf16[64,1,8,4096]{3,2,1,0:T(8,128)(2,1)} %fusion), calls=%async_computation | async-start | bytes 8388608 | tf_op jit(solution)/shard_map/all_to_all | solution.py:68
  191.9 3.6 fusion.23
  195.5 3.4 fusion.20
  198.9 105.7 %all-to-all-done = bf16[64,1,8,4096]{3,2,1,0:T(8,128)(2,1)} async-done(((bf16[64,1,8,4096]{3,2,1,0:T(8,128)(2,1)}), bf16[64,1,8,4096]{3,2,1,0:T(8,128)(2,1)}, u32[]{:S(2)}, u32[]{:S(2)}) %all-to-all-start) | async-done | bytes 4194336 | tf_op jit(solution)/shard_map/all_to_all | solution.py:68
  304.6 3.4 fusion.40
  308.1 1.2 fusion.27
  309.3 3.2 fusion.1
  312.6 91.5 %all-reduce.2.cloned.1.call-done = bf16[64,1,8,4096]{3,2,0,1:T(8,128)(2,1)} async-done(((bf16[64,1,8,4096]{3,2,0,1:T(8,128)(2,1)}), bf16[64,1,8,4096]{3,2,0,1:T(8,128)(2,1)}) %all-reduce.2.cloned.1.call-update) | async-done | bytes 4194320 | tf_op jit(solution)/shard_map/psum | solution.py:73
  404.0 1.9 fusion.35
  405.9 12.8 %all-to-all-start.2 = ((bf16[64,1,8,512]{3,2,1,0:T(8,128)(2,1)}), bf16[64,1,8,512]{3,2,1,0:T(8,128)(2,1)S(1)}, u32[]{:S(2)}, u32[]{:S(2)}) async-start(bf16[64,1,8,512]{3,2,1,0:T(8,128)(2,1)} %fusion.35), calls=%async_computation.2 | async-start | bytes 1048576 | tf_op jit(solution)/shard_map/all_to_all | solution.py:77
  418.8 3.9 fusion.6
  422.7 3.9 fusion.7
  426.6 3.9 fusion.5
  430.6 7.1 %all-to-all-done.2 = bf16[64,1,8,512]{3,2,1,0:T(8,128)(2,1)S(1)} async-done(((bf16[64,1,8,512]{3,2,1,0:T(8,128)(2,1)}), bf16[64,1,8,512]{3,2,1,0:T(8,128)(2,1)S(1)}, u32[]{:S(2)}, u32[]{:S(2)}) %all-to-all-start.2) | async-done | bytes 524320 | tf_op jit(solution)/shard_map/all_to_all | solution.py:77
  437.7 3.8 scatter_custom_fusion
  (32 shorter events, 4.1 us)
Async XLA Ops:
  7.2 184.7 %copy-start = (bf16[1,96,4096]{2,1,0:T(8,128)(2,1)S(1)}, bf16[1,96,4096]{2,1,0:T(8,128)(2,1)}, u32[]{:S(2)}) copy-start(bf16[1,96,4096]{2,1,0:T(8,128)(2,1)} %param.11) | copy-start | bytes 2359300
  33.5 16.4 %copy-start.3 = (f32[48,8]{0,1:T(8,128)S(1)}, f32[48,8]{0,1:T(8,128)}, u32[]{:S(2)}) copy-start(f32[48,8]{0,1:T(8,128)} %param.10) | copy-start | bytes 4612
  33.5 16.7 %copy-start.2 = (bf16[48,512]{1,0:T(8,128)(2,1)S(1)}, bf16[48,512]{1,0:T(8,128)(2,1)}, u32[]{:S(2)}) copy-start(bf16[48,512]{1,0:T(8,128)(2,1)} %param.8) | copy-start | bytes 147460
  33.5 124.5 %all-to-all-start.1 = ((bf16[64,1,8,4096]{3,2,1,0:T(8,128)(2,1)}), bf16[64,1,8,4096]{3,2,1,0:T(8,128)(2,1)}, u32[]{:S(2)}, u32[]{:S(2)}) async-start(bf16[64,1,8,4096]{3,2,1,0:T(8,128)(2,1)} %bitcast_select_fusion), calls=%async_computation.1 | async-start | bytes 8388608 | tf_op jit(solution)/shard_map/all_to_all | solution.py:67
  158.0 146.7 %all-to-all-start = ((bf16[64,1,8,4096]{3,2,1,0:T(8,128)(2,1)}), bf16[64,1,8,4096]{3,2,1,0:T(8,128)(2,1)}, u32[]{:S(2)}, u32[]{:S(2)}) async-start(bf16[64,1,8,4096]{3,2,1,0:T(8,128)(2,1)} %fusion), calls=%async_computation | async-start | bytes 8388608 | tf_op jit(solution)/shard_map/all_to_all | solution.py:68
  191.7 3.8 copy-start.1
  191.7 113.0 %copy-start.4 = (bf16[1,96,4096]{2,1,0:T(8,128)(2,1)S(1)}, bf16[1,96,4096]{2,1,0:T(8,128)(2,1)}, u32[]{:S(2)}) copy-start(bf16[1,96,4096]{2,1,0:T(8,128)(2,1)} %param.13) | copy-start | bytes 2359300
  191.7 212.4 %all-reduce.2.cloned.1.call-start = ((), (), s32[]{:S(2)}) async-start(), calls=%async_computation.3 | async-start | bytes 8388608 | tf_op jit(solution)/shard_map/psum | solution.py:73
  405.9 31.7 %all-to-all-start.2 = ((bf16[64,1,8,512]{3,2,1,0:T(8,128)(2,1)}), bf16[64,1,8,512]{3,2,1,0:T(8,128)(2,1)S(1)}, u32[]{:S(2)}, u32[]{:S(2)}) async-start(bf16[64,1,8,512]{3,2,1,0:T(8,128)(2,1)} %fusion.35), calls=%async_computation.2 | async-start | bytes 1048576 | tf_op jit(solution)/shard_map/all_to_all | solution.py:77
Sparse Core Ops, SparseCore 0:
  312.7 91.2 all-reduce.1
where the time goes:
time: 450 us; the launch traced here: 449 us
  waiting for transfers between devices  288 us (64%)
  starting transfers between devices  63.1 us (14%)
  blocking collectives  27.2 us (6%)
  matrix products  26.7 us (6%)
  other arithmetic  18.7 us (4%)
  between operations  14.2 us (3%)
  local copies, waits for them, and re-layouts  10.5 us (2%)
    all_to_all x1, waiting for transfers between devices, on_device(): lax.all_to_all(sent_d, 'expert', split_axis=0, concat_axis=0, tiled=True)  106 us
    psum x1, waiting for transfers between devices, on_device(): lax.psum(partial_value.astype(jnp.bfloat16), 'tensor').astype(jnp.float32)  91.5 us
    all_to_all x1, waiting for transfers between devices, on_device(): lax.all_to_all(sent_x, 'expert', split_axis=0, concat_axis=0, tiled=True)  84.2 us
    all_to_all x1, starting transfers between devices, on_device(): lax.all_to_all(sent_d, 'expert', split_axis=0, concat_axis=0, tiled=True)  33.7 us
    all_to_all x1, starting transfers between devices, on_device(): lax.all_to_all(sent_x, 'expert', split_axis=0, concat_axis=0, tiled=True)  16.3 us
    all_gather x1, blocking collectives, on_device(): lax.all_gather(tokens, 'tensor', axis=1, tiled=True)  13.7 us
    all_gather x1, blocking collectives, on_device(): lax.all_gather(cotangent, 'tensor', axis=1, tiled=True)  13.5 us
    all_to_all x1, starting transfers between devices, on_device(): lax.all_to_all(returned, 'expert', split_axis=0, concat_axis=0, tiled=True)  12.8 us
  transfers between devices with their start and end apart: 4, of which 4 were waited for; matrix products, arithmetic and copies ran while one was open for 6% of the time, Pallas kernels for 0%

commit v1 on v0

--- a/solution.py
+++ b/solution.py
@@ -4,6 +4,11 @@
 from jax.sharding import PartitionSpec as P
 
 TOP = 8
+
+
+def exchange_gather(x, axis, dim):
+    repeated = jnp.stack([x] * lax.axis_size(axis))
+    return jnp.concatenate(lax.all_to_all(repeated, axis, 0, 0), axis=dim)
 
 
 def expert_backward(rows_x, rows_d, w_gate, w_up, w_down):
@@ -56,7 +61,7 @@
     owner = jnp.sum(jnp.where(by_token, token_iota[None, :], 0), axis=1)
     slot_weight = jnp.sum(jnp.sum(jnp.where(matches, gate_values[None, :, :], 0.0), axis=2), axis=1)
     full_x, full_d = (
-        lax.all_gather(tokens, "tensor", axis=1, tiled=True),
+        exchange_gather(tokens, "tensor", 1),
         lax.all_gather(cotangent, "tensor", axis=1, tiled=True),
     )
     sent_x = jnp.where(occupied[:, None], full_x[owner], jnp.zeros((), jnp.bfloat16))

time: 450 us -> 447 us (level)
  blocking collectives: 27.2 us -> 14.2 us
  waiting for transfers between devices: 288 us -> 299 us
    psum x1, waiting for transfers between devices: 91.5 us -> 107 us  [on_device(): lax.psum(partial_value.astype(jnp.bfloat16), 'tensor').astype(jnp.float32)]
    all_gather x1 -> x0, blocking collectives: 13.7 us -> none  [on_device(): lax.all_gather(tokens, 'tensor', axis=1, tiled=True)]
    all_to_all x1, waiting for transfers between devices: 106 us -> 99 us  [on_device(): lax.all_to_all(sent_d, 'expert', split_axis=0, concat_axis=0, tiled=True)]
    all_to_all x1, starting transfers between devices: 33.7 us -> 27.5 us  [on_device(): lax.all_to_all(sent_d, 'expert', split_axis=0, concat_axis=0, tiled=True)]
    all_to_all x0 -> x1, starting transfers between devices: none -> 5.09 us  [exchange_gather(): return jnp.concatenate(lax.all_to_all(repeated, axis, 0, 0), axis=dim)]
  transfers between devices with their start and end apart: 4 -> 5, of which waited for: 4 -> 5; matrix products, arithmetic and copies ran while one was open for 6% -> 7% of each run, Pallas kernels for 0% -> 0%
where the time goes in v1:
time: 447 us; the launch traced here: 446 us
  waiting for transfers between devices  299 us (67%)
  starting transfers between devices  62 us (14%)
  matrix products  26.7 us (6%)
  other arithmetic  18.7 us (4%)
  blocking collectives  14.2 us (3%)
  between operations  14.2 us (3%)
  local copies, waits for them, and re-layouts  12.1 us (3%)
    psum x1, waiting for transfers between devices, on_device(): lax.psum(partial_value.astype(jnp.bfloat16), 'tensor').astype(jnp.float32)  107 us
    all_to_all x1, waiting for transfers between devices, on_device(): lax.all_to_all(sent_d, 'expert', split_axis=0, concat_axis=0, tiled=True)  99 us
    all_to_all x1, waiting for transfers between devices, on_device(): lax.all_to_all(sent_x, 'expert', split_axis=0, concat_axis=0, tiled=True)  83.2 us
    all_to_all x1, starting transfers between devices, on_device(): lax.all_to_all(sent_d, 'expert', split_axis=0, concat_axis=0, tiled=True)  27.5 us
    all_to_all x1, starting transfers between devices, on_device(): lax.all_to_all(sent_x, 'expert', split_axis=0, concat_axis=0, tiled=True)  16.3 us
    all_gather x1, blocking collectives, on_device(): lax.all_gather(cotangent, 'tensor', axis=1, tiled=True)  14.2 us
    all_to_all x1, starting transfers between devices, on_device(): lax.all_to_all(returned, 'expert', split_axis=0, concat_axis=0, tiled=True)  12.8 us
  transfers between devices with their start and end apart: 5, of which 5 were waited for; matrix products, arithmetic and copies ran while one was open for 7% of the time, Pallas kernels for 0%

profile of v1, /device:TPU:15, one launch (start us, length us, event | category | flops | bytes accessed | tf_op | source)
XLA Modules:
  0.0 446.5 jit_solution(2468524915834146209)
XLA Ops:
  7.2 1.6 stack.2
  8.8 5.1 %all-to-all-start.1 = ((bf16[8,48,512]{2,1,0:T(8,128)(2,1)}), bf16[8,48,512]{2,1,0:T(8,128)(2,1)S(1)}, u32[]{:S(2)}, u32[]{:S(2)}) async-start(bf16[8,48,512]{2,1,0:T(8,128)(2,1)} %stack.2), calls=%async_computation.1 | async-start | bytes 786432 | tf_op jit(solution)/shard_map/all_to_all | solution.py:11
  17.6 2.7 all-to-all-done.1
  20.3 4.4 gather_fusion.1
  24.7 4.5 %bitcast_select_fusion = bf16[64,1,8,4096]{3,2,1,0:T(8,128)(2,1)} fusion(bf16[512,4096]{1,0:T(8,128)(2,1)} %gather_fusion.1, pred[64,8]{1,0:T(8,128)(4,1)S(1)} %broadcast_in_dim.73), kind=kLoop, calls=%fused_computation.16 | loop fusion | flops 2097152 | bytes 8389120 | tf_op jit(solution)/shard_map/jit(_where)/select_n | solution.py:67
  29.2 16.3 %all-to-all-start.2 = ((bf16[64,1,8,4096]{3,2,1,0:T(8,128)(2,1)}), bf16[64,1,8,4096]{3,2,1,0:T(8,128)(2,1)}, u32[]{:S(2)}, u32[]{:S(2)}) async-start(bf16[64,1,8,4096]{3,2,1,0:T(8,128)(2,1)} %bitcast_select_fusion), calls=%async_computation.2 | async-start | bytes 8388608 | tf_op jit(solution)/shard_map/all_to_all | solution.py:72
  45.9 14.2 %all_gather.3 = bf16[48,4096]{1,0:T(8,128)(2,1)S(1)} all-gather(bf16[48,512]{1,0:T(8,128)(2,1)S(1)} %copy-done.2), channel_id=1, replica_groups=mesh['expert'=64,'tensor'=8] {'tensor'}, dimensions={1}, use_global_device_ids=true | all-gather | bytes 442368 | tf_op jit(solution)/shard_map/all_gather | solution.py:65
  60.1 4.4 gather_fusion
  64.5 5.6 %fusion = bf16[64,1,8,4096]{3,2,1,0:T(8,128)(2,1)} fusion(bf16[512,4096]{1,0:T(8,128)(2,1)} %gather_fusion, f32[64,8]{1,0:T(8,128)S(1)} %mul.57), kind=kLoop, calls=%fused_computation.4 | loop fusion | flops 6291456 | bytes 8390656 | tf_op jit(solution)/shard_map/convert_element_type | solution.py:68
  70.1 83.2 %all-to-all-done.2 = bf16[64,1,8,4096]{3,2,1,0:T(8,128)(2,1)} async-done(((bf16[64,1,8,4096]{3,2,1,0:T(8,128)(2,1)}), bf16[64,1,8,4096]{3,2,1,0:T(8,128)(2,1)}, u32[]{:S(2)}, u32[]{:S(2)}) %all-to-all-start.2) | async-done | bytes 4194336 | tf_op jit(solution)/shard_map/all_to_all | solution.py:72
  153.3 27.5 %all-to-all-start = ((bf16[64,1,8,4096]{3,2,1,0:T(8,128)(2,1)}), bf16[64,1,8,4096]{3,2,1,0:T(8,128)(2,1)}, u32[]{:S(2)}, u32[]{:S(2)}) async-start(bf16[64,1,8,4096]{3,2,1,0:T(8,128)(2,1)} %fusion), calls=%async_computation | async-start | bytes 8388608 | tf_op jit(solution)/shard_map/all_to_all | solution.py:73
  181.1 3.6 fusion.23
  184.7 3.4 fusion.20
  188.1 99.0 %all-to-all-done = bf16[64,1,8,4096]{3,2,1,0:T(8,128)(2,1)} async-done(((bf16[64,1,8,4096]{3,2,1,0:T(8,128)(2,1)}), bf16[64,1,8,4096]{3,2,1,0:T(8,128)(2,1)}, u32[]{:S(2)}, u32[]{:S(2)}) %all-to-all-start) | async-done | bytes 4194336 | tf_op jit(solution)/shard_map/all_to_all | solution.py:73
  287.1 3.4 fusion.40
  291.8 3.2 fusion.1
  295.0 106.6 %all-reduce.2.cloned.1.call-done = bf16[64,1,8,4096]{3,2,0,1:T(8,128)(2,1)} async-done(((bf16[64,1,8,4096]{3,2,0,1:T(8,128)(2,1)}), bf16[64,1,8,4096]{3,2,0,1:T(8,128)(2,1)}) %all-reduce.2.cloned.1.call-update) | async-done | bytes 4194320 | tf_op jit(solution)/shard_map/psum | solution.py:78
  401.6 1.9 fusion.35
  403.5 12.8 %all-to-all-start.3 = ((bf16[64,1,8,512]{3,2,1,0:T(8,128)(2,1)}), bf16[64,1,8,512]{3,2,1,0:T(8,128)(2,1)S(1)}, u32[]{:S(2)}, u32[]{:S(2)}) async-start(bf16[64,1,8,512]{3,2,1,0:T(8,128)(2,1)} %fusion.35), calls=%async_computation.3 | async-start | bytes 1048576 | tf_op jit(solution)/shard_map/all_to_all | solution.py:82
  416.4 3.9 fusion.6
  420.3 3.9 fusion.7
  424.2 3.9 fusion.5
  428.2 7.1 %all-to-all-done.3 = bf16[64,1,8,512]{3,2,1,0:T(8,128)(2,1)S(1)} async-done(((bf16[64,1,8,512]{3,2,1,0:T(8,128)(2,1)}), bf16[64,1,8,512]{3,2,1,0:T(8,128)(2,1)S(1)}, u32[]{:S(2)}, u32[]{:S(2)}) %all-to-all-start.3) | async-done | bytes 524320 | tf_op jit(solution)/shard_map/all_to_all | solution.py:82
  435.3 3.8 scatter_custom_fusion
  (35 shorter events, 6.1 us)
Async XLA Ops:
  7.2 173.9 %copy-start = (bf16[1,96,4096]{2,1,0:T(8,128)(2,1)S(1)}, bf16[1,96,4096]{2,1,0:T(8,128)(2,1)}, u32[]{:S(2)}) copy-start(bf16[1,96,4096]{2,1,0:T(8,128)(2,1)} %param.11) | copy-start | bytes 2359300
  8.8 11.5 %all-to-all-start.1 = ((bf16[8,48,512]{2,1,0:T(8,128)(2,1)}), bf16[8,48,512]{2,1,0:T(8,128)(2,1)S(1)}, u32[]{:S(2)}, u32[]{:S(2)}) async-start(bf16[8,48,512]{2,1,0:T(8,128)(2,1)} %stack.2), calls=%async_computation.1 | async-start | bytes 786432 | tf_op jit(solution)/shard_map/all_to_all | solution.py:11
  29.2 16.4 %copy-start.3 = (f32[48,8]{0,1:T(8,128)S(1)}, f32[48,8]{0,1:T(8,128)}, u32[]{:S(2)}) copy-start(f32[48,8]{0,1:T(8,128)} %param.10) | copy-start | bytes 4612
  29.2 16.7 %copy-start.2 = (bf16[48,512]{1,0:T(8,128)(2,1)S(1)}, bf16[48,512]{1,0:T(8,128)(2,1)}, u32[]{:S(2)}) copy-start(bf16[48,512]{1,0:T(8,128)(2,1)} %param.8) | copy-start | bytes 147460
  29.2 124.1 %all-to-all-start.2 = ((bf16[64,1,8,4096]{3,2,1,0:T(8,128)(2,1)}), bf16[64,1,8,4096]{3,2,1,0:T(8,128)(2,1)}, u32[]{:S(2)}, u32[]{:S(2)}) async-start(bf16[64,1,8,4096]{3,2,1,0:T(8,128)(2,1)} %bitcast_select_fusion), calls=%async_computation.2 | async-start | bytes 8388608 | tf_op jit(solution)/shard_map/all_to_all | solution.py:72
  153.3 133.8 %all-to-all-start = ((bf16[64,1,8,4096]{3,2,1,0:T(8,128)(2,1)}), bf16[64,1,8,4096]{3,2,1,0:T(8,128)(2,1)}, u32[]{:S(2)}, u32[]{:S(2)}) async-start(bf16[64,1,8,4096]{3,2,1,0:T(8,128)(2,1)} %fusion), calls=%async_computation | async-start | bytes 8388608 | tf_op jit(solution)/shard_map/all_to_all | solution.py:73
  180.8 3.8 copy-start.1
  180.8 106.3 %copy-start.4 = (bf16[1,96,4096]{2,1,0:T(8,128)(2,1)S(1)}, bf16[1,96,4096]{2,1,0:T(8,128)(2,1)}, u32[]{:S(2)}) copy-start(bf16[1,96,4096]{2,1,0:T(8,128)(2,1)} %param.13) | copy-start | bytes 2359300
  180.8 220.8 %all-reduce.2.cloned.1.call-start = ((), (), s32[]{:S(2)}) async-start(), calls=%async_computation.4 | async-start | bytes 8388608 | tf_op jit(solution)/shard_map/psum | solution.py:78
  403.5 31.7 %all-to-all-start.3 = ((bf16[64,1,8,512]{3,2,1,0:T(8,128)(2,1)}), bf16[64,1,8,512]{3,2,1,0:T(8,128)(2,1)S(1)}, u32[]{:S(2)}, u32[]{:S(2)}) async-start(bf16[64,1,8,512]{3,2,1,0:T(8,128)(2,1)} %fusion.35), calls=%async_computation.3 | async-start | bytes 1048576 | tf_op jit(solution)/shard_map/all_to_all | solution.py:82
Sparse Core Ops, SparseCore 0:
  295.1 106.4 all-reduce.1
